TPU v7x, 256 devices: a whole 4x4x8 slice. The times are simulated.
256 devices in a mesh: space: 16 (over y, x), blk: 16 (over z, core).
Axes of the slice: x: 4, y: 4, z: 8, core: 2. Of those that a mesh axis runs over, the one named last changes fastest.
Arguments:
- snapshots: bfloat16 [64, 512, 3, 8192], P('blk', None, None, 'space'), may hold values from -6 to 6
- quadrature: float32 [8192], P('space'), may hold values from 0.2 to 5
- omega: float32 [16, 2, 64, 16], replicated, may hold values from -6 to 6
Outputs:
- modes: float32 [16, 2, 16, 3, 8192], P('blk', None, None, None, 'space')
- energies: float32 [16, 16], replicated
All inputs are finite; a program needn't handle non-finite values.
Results may differ from a plain program's by a relative error of at most 0.0051.
Values may be sent and summed in bfloat16 or wider, within the bound.
A program may use at most 64 MiB of HBM per device.

v0:
```python
import functools
import math

import jax
import jax.numpy as jnp
import numpy as np
from jax import lax
from jax.experimental import pallas as pl
from jax.experimental.pallas import tpu as pltpu
from jax.sharding import PartitionSpec as P

NT = 512
NF = 16
RANK = 16
COMP = 3
ITERS = 2
NS_STEPS = 14
SHARE = 4
ROWS = 2 * SHARE
HIGHEST = lax.Precision.HIGHEST
MESH = pl.DeviceIdType.MESH


def dft_table():
    sample = np.arange(NT)
    harmonic = np.arange(1, NF + 1)
    phases = 2.0 * math.pi / NT * (harmonic[:, None] * sample[None, :] % NT)
    window = 0.5 - 0.5 * np.cos(2.0 * math.pi / NT * sample)
    factor = 1.0 / np.sqrt(np.sum(window * window))
    table = np.concatenate([window * np.cos(phases), -window * np.sin(phases)], 0) * factor
    return table.astype(np.float32).astype(jnp.bfloat16)


def iota(shape, dim):
    return lax.broadcasted_iota(jnp.int32, shape, dim)


def mm(left, right, precision=HIGHEST):
    return jnp.dot(left, right, precision=precision, preferred_element_type=jnp.float32)


def mm_nt(left, right, precision=HIGHEST):
    return lax.dot_general(
        left, right, (((1,), (1,)), ((), ())), precision=precision, preferred_element_type=jnp.float32
    )


def pieces(value):
    high = value.astype(jnp.bfloat16).astype(jnp.float32)
    rest = value - high
    mid = rest.astype(jnp.bfloat16).astype(jnp.float32)
    return high, mid, rest - mid


def left_form(value):
    high, mid, low = pieces(value)
    lane = iota(value.shape, 1)
    near = jnp.where(lane < 96, high, mid).astype(jnp.bfloat16)
    far = jnp.where(lane < 32, mid, jnp.where(lane < 64, low, 0.0)).astype(jnp.bfloat16)
    return jnp.concatenate([near, far], axis=1)


def right_form(value):
    high, mid, low = (piece.astype(jnp.bfloat16) for piece in pieces(value))
    return jnp.concatenate([high, mid, low, high, mid, high, high, high], axis=0)


def wide(left, right):
    return jnp.dot(left, right, preferred_element_type=jnp.float32)


def inverse_root(joined):
    shape = joined.shape
    eye = jnp.where(iota(shape, 0) == iota(shape, 1) % (2 * RANK), 1.0, 0.0).astype(jnp.float32)
    squared = wide(left_form(joined), right_form(joined))
    own = jnp.where(iota(shape, 1) < 2 * RANK, joined * joined, 0.0)
    norm = jnp.sqrt(jnp.sum(jnp.sum(own, axis=0, keepdims=True), axis=1, keepdims=True))
    inv_norm = 1.0 / norm
    first = joined * inv_norm
    inverse_state = 1.5 * eye - 0.5 * first
    root_state = 1.5 * first - 0.5 * (squared * inv_norm * inv_norm)
    for step in range(1, NS_STEPS):
        factor = 1.5 * eye - 0.5 * wide(left_form(inverse_state), right_form(root_state))
        if step < NS_STEPS - 1:
            root_state = wide(left_form(root_state), right_form(factor))
        inverse_state = wide(left_form(factor), right_form(inverse_state))
    return inverse_state * (1.0 / jnp.sqrt(norm))


def kernel(
    groups,
    shares,
    snap_hbm,
    table_hbm,
    quad_hbm,
    omega_hbm,
    modes_hbm,
    energy_out,
    snap,
    table,
    quad,
    omega,
    filt,
    outgoing,
    spectra,
    gram_part,
    gram_in,
    gram,
    energy,
    modes,
    small_sem,
    load_sem,
    send_sem,
    recv_sem,
    gram_send,
    gram_recv,
    row_send,
    row_recv,
    energy_send,
    energy_recv,
    store_sem,
):
    group = lax.axis_index("blk")
    share = lax.axis_index("space")
    block_total = groups * SHARE
    lanes = groups * ROWS
    width = snap.shape[2]

    small = [
        pltpu.make_async_copy(table_hbm, table, small_sem.at[0]),
        pltpu.make_async_copy(quad_hbm, quad, small_sem.at[1]),
        pltpu.make_async_copy(omega_hbm.at[group], omega, small_sem.at[2]),
    ]
    for copy in small:
        copy.start()
    loads = [
        [
            pltpu.make_async_copy(snap_hbm.at[b, c], snap.at[c, pl.ds(b * NT, NT)], load_sem.at[c, b])
            for b in range(SHARE)
        ]
        for c in range(COMP)
    ]
    for per_comp in loads:
        for copy in per_comp:
            copy.start()

    barrier = pltpu.get_barrier_semaphore()

    def greet_group(i, carry):
        pl.semaphore_signal(
            barrier, inc=1, device_id=(share, lax.rem(group + i, groups)), device_id_type=MESH
        )
        return carry

    def greet_share(i, carry):
        pl.semaphore_signal(
            barrier, inc=1, device_id=(lax.rem(share + i, shares), group), device_id_type=MESH
        )
        return carry

    lax.fori_loop(1, groups, greet_group, 0)
    lax.fori_loop(1, shares, greet_share, 0)

    for copy in small:
        copy.wait()

    row = iota((lanes, 2 * NF), 0)
    column = iota((lanes, 2 * NF), 1)
    wanted = row // ROWS + NF * (row // SHARE % 2)
    for b in range(SHARE):
        chosen = jnp.where((column == wanted) & (row % SHARE == b), 1.0, 0.0).astype(jnp.bfloat16)
        filt[:, b * NT : (b + 1) * NT] = wide(chosen, table[...]).astype(jnp.bfloat16)
    root_weight = jnp.sqrt(quad[...])

    def block_copy(c, target):
        return pltpu.make_async_remote_copy(
            src_ref=outgoing.at[c, target],
            dst_ref=spectra.at[c, group],
            send_sem=send_sem.at[c],
            recv_sem=recv_sem.at[c],
            device_id=(share, target),
            device_id_type=MESH,
        )

    for c in range(COMP):
        for copy in loads[c]:
            copy.wait()
        weighted = (wide(filt[...], snap[c]) * root_weight).astype(jnp.bfloat16)
        outgoing[c] = weighted.reshape(groups, ROWS, width)
        if c == 0:
            pl.semaphore_wait(barrier, groups + shares - 2)

        def send_block(i, carry):
            block_copy(c, lax.rem(group + i, groups)).start()
            return carry

        lax.fori_loop(1, groups, send_block, 0)
        spectra[c, group] = outgoing[c, group]

    block = iota((block_total, lanes), 0)
    lane = iota((block_total, lanes), 1)
    same_block = block == lane // ROWS * SHARE + lane % SHARE
    is_real = lane // SHARE % 2 == 0
    real_lanes = jnp.where(same_block & is_real, 1.0, 0.0).astype(jnp.float32)
    imag_lanes = jnp.where(same_block & ~is_real, 1.0, 0.0).astype(jnp.float32)
    start_re, start_im = omega[0], omega[1]
    coef = mm(jnp.concatenate([start_re, start_im], 0), real_lanes) + mm(
        jnp.concatenate([-start_im, start_re], 0), imag_lanes
    )

    def whole(c):
        return spectra.at[c, pl.ds(0, groups - 1)]

    total = jnp.zeros((lanes, lanes), jnp.float32)
    for c in range(COMP):
        pltpu.make_async_remote_copy(
            src_ref=whole(c),
            dst_ref=whole(c),
            send_sem=send_sem.at[c],
            recv_sem=recv_sem.at[c],
            device_id=(share, lax.rem(group + 1, groups)),
            device_id_type=MESH,
        ).wait_recv()
        rows = spectra[c].reshape(lanes, width)
        total = total + mm_nt(rows, rows, None)

    gram_part[...] = total.reshape(shares, ROWS, lanes)

    def gram_copy(source, landing, peer, send, recv):
        return pltpu.make_async_remote_copy(
            src_ref=source,
            dst_ref=landing,
            send_sem=send,
            recv_sem=recv,
            device_id=(peer, group),
            device_id_type=MESH,
        )

    def send_part(i, carry):
        peer = lax.rem(share + i, shares)
        gram_copy(gram_part.at[peer], gram_in.at[share], peer, gram_send, gram_recv).start()
        return carry

    lax.fori_loop(1, shares, send_part, 0)
    gram_in[share] = gram_part[share]
    others = pl.ds(0, shares - 1)
    next_share = lax.rem(share + 1, shares)
    gram_copy(gram_in.at[others], gram_in.at[others], next_share, gram_send, gram_recv).wait_recv()
    mine = jnp.sum(gram_in[...], axis=0)
    rolled = pltpu.roll(mine, SHARE, 0)
    lane = iota((ROWS, lanes), 1) // SHARE % 2
    partner = jnp.where(
        lane == 0, pltpu.roll(rolled, lanes - SHARE, 1), pltpu.roll(rolled, SHARE, 1)
    )
    partner = jnp.where(lane == iota((ROWS, lanes), 0) // SHARE, partner, -partner)
    gram[share] = (mine + partner) * (1.0 / (COMP * width * shares))

    def send_row(i, carry):
        gram_copy(gram.at[share], gram.at[share], lax.rem(share + i, shares), row_send, row_recv).start()
        return carry

    lax.fori_loop(1, shares, send_row, 0)
    gram_copy(gram.at[others], gram.at[others], next_share, row_send, row_recv).wait_recv()
    matrix = gram[...].reshape(lanes, lanes)

    nxt = mm(coef, matrix)
    image = mm(nxt, matrix)
    for step in range(ITERS):
        joined = mm_nt(nxt, jnp.concatenate([image] * 4, 0))
        if step < ITERS - 1:
            further = mm(image, matrix)
            left = left_form(inverse_root(joined))
            nxt, image = wide(left, right_form(image)), wide(left, right_form(further))
        else:
            left = left_form(inverse_root(joined))
            coef, final = wide(left, right_form(nxt)), wide(left, right_form(image))

    squares = mm_nt(jnp.ones((ROWS, lanes), jnp.float32), jnp.concatenate([final * final] * 4, 0))
    energy[group] = squares[:1, :]

    def energy_copy(source, landing, peer):
        return pltpu.make_async_remote_copy(
            src_ref=source,
            dst_ref=landing,
            send_sem=energy_send,
            recv_sem=energy_recv,
            device_id=(share, peer),
            device_id_type=MESH,
        )

    def send_energy(i, carry):
        energy_copy(energy.at[group], energy.at[group], lax.rem(group + i, groups)).start()
        return carry

    lax.fori_loop(1, groups, send_energy, 0)

    coef_low = coef.astype(jnp.bfloat16)
    inv_weight = 1.0 / root_weight
    for c in range(COMP):
        out = wide(coef_low, spectra[c].reshape(lanes, width)) * inv_weight
        modes[0, c] = out[:RANK]
        modes[1, c] = out[RANK:]
    store = pltpu.make_async_copy(modes, modes_hbm, store_sem)
    store.start()

    other_groups = pl.ds(0, groups - 1)
    next_group = lax.rem(group + 1, groups)
    energy_copy(energy.at[other_groups], energy.at[other_groups], next_group).wait()
    energy_out[...] = energy[...].reshape(groups, 128)[:, :RANK]
    gram_copy(gram_in.at[others], gram_in.at[others], next_share, gram_send, gram_recv).wait_send()
    gram_copy(gram.at[others], gram.at[others], next_share, row_send, row_recv).wait_send()
    for c in range(COMP):
        pltpu.make_async_remote_copy(
            src_ref=whole(c),
            dst_ref=whole(c),
            send_sem=send_sem.at[c],
            recv_sem=recv_sem.at[c],
            device_id=(share, next_group),
            device_id_type=MESH,
        ).wait_send()
    store.wait()


def per_device(snapshots, quadrature, omega):
    groups, shares = lax.axis_size("blk"), lax.axis_size("space")
    width = snapshots.shape[3]
    lanes = groups * ROWS
    any_space = pl.BlockSpec(memory_space=pl.ANY)
    dma = pltpu.SemaphoreType.DMA
    modes, energies = pl.pallas_call(
        functools.partial(kernel, groups, shares),
        out_shape=(
            jax.ShapeDtypeStruct((2, COMP, RANK, width), jnp.float32),
            jax.ShapeDtypeStruct((NF, RANK), jnp.float32),
        ),
        in_specs=[any_space] * 4,
        out_specs=(any_space, pl.BlockSpec(memory_space=pltpu.VMEM)),
        scratch_shapes=[
            pltpu.VMEM((COMP, SHARE * NT, width), jnp.bfloat16),
            pltpu.VMEM((2 * NF, NT), jnp.bfloat16),
            pltpu.VMEM((1, width), jnp.float32),
            pltpu.VMEM((2, RANK, groups * SHARE), jnp.float32),
            pltpu.VMEM((lanes, SHARE * NT), jnp.bfloat16),
            pltpu.VMEM((COMP, groups, ROWS, width), jnp.bfloat16),
            pltpu.VMEM((COMP, groups, ROWS, width), jnp.bfloat16),
            pltpu.VMEM((shares, ROWS, lanes), jnp.float32),
            pltpu.VMEM((shares, ROWS, lanes), jnp.float32),
            pltpu.VMEM((shares, ROWS, lanes), jnp.float32),
            pltpu.VMEM((groups, 1, 128), jnp.float32),
            pltpu.VMEM((2, COMP, RANK, width), jnp.float32),
            dma((3,)),
            dma((COMP, SHARE)),
            dma((COMP,)),
            dma((COMP,)),
            dma(()),
            dma(()),
            dma(()),
            dma(()),
            dma(()),
            dma(()),
            dma(()),
        ],
        compiler_params=pltpu.CompilerParams(
            collective_id=0, has_side_effects=True, vmem_limit_bytes=40 << 20
        ),
    )(
        jnp.transpose(snapshots, (0, 2, 1, 3)),
        jnp.asarray(dft_table()),
        quadrature.reshape(1, width),
        jnp.transpose(omega, (0, 1, 3, 2)),
    )
    return jnp.transpose(modes, (0, 2, 1, 3))[None], energies


def solution(mesh):
    in_specs = (P("blk", None, None, "space"), P("space"), P())
    out_specs = (P("blk", None, None, None, "space"), P())
    return jax.shard_map(
        per_device, mesh=mesh, in_specs=in_specs, out_specs=out_specs, check_vma=False
    )
```

profile of v0, /device:TPU:1, one launch (start us, length us, event | category | flops | bytes accessed | tf_op | source)
XLA Modules:
  0.0 53.0 jit_solution(14388532488683598004)
XLA Ops:
  0.6 0.0 copy-start
  0.6 2.8 %copy-done = bf16[4,512,3,512]{3,1,2,0:T(8,128)(2,1)S(1)} copy-done((bf16[4,512,3,512]{3,1,2,0:T(8,128)(2,1)S(1)}, bf16[4,512,3,512]{3,1,2,0:T(8,128)(2,1)}, u32[]{:S(2)}) %copy-start) | copy-done | bytes 6291480
  3.4 0.0 copy-start.1
  3.4 0.9 %copy-done.1 = f32[16,2,64,16]{2,3,1,0:T(8,128)S(1)} copy-done((f32[16,2,64,16]{2,3,1,0:T(8,128)S(1)}, f32[16,2,64,16]{2,3,1,0:T(8,128)}, u32[]{:S(2)}) %copy-start.1) | copy-done | bytes 131096
  4.4 0.0 copy-start.2
  4.4 0.8 %copy-done.2 = bf16[32,512]{1,0:T(8,128)(2,1)S(1)} copy-done((bf16[32,512]{1,0:T(8,128)(2,1)S(1)}, bf16[32,512]{1,0:T(8,128)(2,1)}, u32[]{:S(2)}) %copy-start.2) | copy-done | bytes 32792
  5.1 0.0 copy-start.3
  5.1 0.7 %copy-done.3 = f32[512]{0:T(512)S(1)} copy-done((f32[512]{0:T(512)S(1)}, f32[512]{0:T(512)}, u32[]{:S(2)}) %copy-start.3) | copy-done | bytes 2072
  5.8 45.9 %shard_map.59 = (f32[2,3,16,512]{3,2,1,0:T(8,128)S(1)}, f32[16,16]{1,0:T(8,128)S(1)}) custom-call(bf16[4,3,512,512]{3,2,1,0:T(8,128)(2,1)S(1)} %bitcast.6, bf16[32,512]{1,0:T(8,128)(2,1)S(1)} %copy-done.2, f32[1,512]{1,0:T(1,128)S(1)} %bitcast.9, f32[16,2,16,64]{3,2,1,0:T(8,128)S(1)} %bitcast.7), custom_call_target="tpu_custom_call" | custom-call | tf_op jit(solution)/shard_map/pallas_call | solution.py:330
  51.7 0.7 %copy.8 = f32[1,2,16,3,512]{4,2,3,1,0:T(8,128)} copy(f32[1,2,16,3,512]{4,2,3,1,0:T(8,128)S(1)} %bitcast.8) | data formatting | bytes 393216
  52.4 0.6 %copy.9 = f32[16,16]{1,0:T(8,128)} copy(f32[16,16]{1,0:T(8,128)S(1)} %get-tuple-element.9) | data formatting | bytes 2048
Async XLA Ops:
  0.6 2.8 %copy-start = (bf16[4,512,3,512]{3,1,2,0:T(8,128)(2,1)S(1)}, bf16[4,512,3,512]{3,1,2,0:T(8,128)(2,1)}, u32[]{:S(2)}) copy-start(bf16[4,512,3,512]{3,1,2,0:T(8,128)(2,1)} %param.4) | copy-start | bytes 18874372
  3.4 0.9 %copy-start.1 = (f32[16,2,64,16]{2,3,1,0:T(8,128)S(1)}, f32[16,2,64,16]{2,3,1,0:T(8,128)}, u32[]{:S(2)}) copy-start(f32[16,2,64,16]{2,3,1,0:T(8,128)} %param.6) | copy-start | bytes 393220
  4.4 0.8 %copy-start.2 = (bf16[32,512]{1,0:T(8,128)(2,1)S(1)}, bf16[32,512]{1,0:T(8,128)(2,1)}, u32[]{:S(2)}) copy-start(bf16[32,512]{1,0:T(8,128)(2,1)} %constant.2.clone.table_hbm) | copy-start | bytes 98308
  5.1 0.7 %copy-start.3 = (f32[512]{0:T(512)S(1)}, f32[512]{0:T(512)}, u32[]{:S(2)}) copy-start(f32[512]{0:T(512)} %param.5) | copy-start | bytes 6148
where the time goes:
time: 53.2 us; the launch traced here: 53 us
  Pallas kernels  45.9 us (86%)
  local copies, waits for them, and re-layouts  6.44 us (12%)
  between operations  0.65 us (1%)
    pallas_call x1, Pallas kernels, per_device(): pl.pallas_call(functools.partial(kernel, groups, shares), out_shape=(jax....  45.9 us
    unnamed x10, local copies, waits for them, and re-layouts  6.44 us

commit v1 on v0

--- a/solution.py
+++ b/solution.py
@@ -31,6 +31,15 @@
     return table.astype(np.float32).astype(jnp.bfloat16)
 
 
+def far_first(count):
+    return sorted(range(1, count), key=lambda step: -min(step, count - step))
+
+
+def grid_far_first(side):
+    offsets = [(i, j) for i in range(side) for j in range(side) if i or j]
+    return sorted(offsets, key=lambda o: -min(o[0], side - o[0]) - min(o[1], side - o[1]))
+
+
 def iota(shape, dim):
     return lax.broadcasted_iota(jnp.int32, shape, dim)
 
@@ -69,22 +78,76 @@
     return jnp.dot(left, right, preferred_element_type=jnp.float32)
 
 
-def inverse_root(joined):
-    shape = joined.shape
-    eye = jnp.where(iota(shape, 0) == iota(shape, 1) % (2 * RANK), 1.0, 0.0).astype(jnp.float32)
-    squared = wide(left_form(joined), right_form(joined))
-    own = jnp.where(iota(shape, 1) < 2 * RANK, joined * joined, 0.0)
-    norm = jnp.sqrt(jnp.sum(jnp.sum(own, axis=0, keepdims=True), axis=1, keepdims=True))
-    inv_norm = 1.0 / norm
-    first = joined * inv_norm
-    inverse_state = 1.5 * eye - 0.5 * first
-    root_state = 1.5 * first - 0.5 * (squared * inv_norm * inv_norm)
-    for step in range(1, NS_STEPS):
-        factor = 1.5 * eye - 0.5 * wide(left_form(inverse_state), right_form(root_state))
-        if step < NS_STEPS - 1:
-            root_state = wide(left_form(root_state), right_form(factor))
-        inverse_state = wide(left_form(factor), right_form(inverse_state))
-    return inverse_state * (1.0 / jnp.sqrt(norm))
+def lane_sum_free(value):
+    for shift in (4, 2, 1):
+        value = value + pltpu.roll(value, shift, 0)
+    return value
+
+
+def take(value, index):
+    return jnp.take_along_axis(value, index, axis=1)
+
+
+class Flat:
+    def __init__(self):
+        sub, lane = iota((8, 128), 0), iota((8, 128), 1)
+        self.left_index = [lane // RANK * RANK + 8 * half + sub for half in range(2)]
+        self.right_index = sub * RANK + lane % RANK
+        self.own_row = lane // RANK == sub
+        zero = jnp.zeros((8, 128), jnp.float32)
+        self.eye = [
+            jnp.where(lane // RANK + 8 * half == lane % RANK, 1.0, 0.0).astype(jnp.float32)
+            for half in range(2)
+        ] + [zero, zero]
+
+    def left(self, mat):
+        return [[[take(mat[2 * p + h], self.left_index[k]) for k in range(2)] for h in range(2)] for p in range(2)]
+
+    def right(self, mat):
+        return [[take(mat[2 * p + k], self.right_index) for k in range(2)] for p in range(2)]
+
+    def product(self, left, right):
+        out = []
+        for p in range(2):
+            for h in range(2):
+                if p == 0:
+                    terms = [left[0][h][k] * right[0][k] - left[1][h][k] * right[1][k] for k in range(2)]
+                else:
+                    terms = [left[0][h][k] * right[1][k] + left[1][h][k] * right[0][k] for k in range(2)]
+                out.append(lane_sum_free(terms[0] + terms[1]))
+        return out
+
+    def from_rows(self, rows):
+        return [
+            lane_sum_free(jnp.where(self.own_row, rows[8 * part : 8 * part + 8], 0.0))
+            for part in range(4)
+        ]
+
+    def embedded(self, mat):
+        real = jnp.concatenate([take(mat[0], self.right_index), take(mat[1], self.right_index)], 0)
+        imag = jnp.concatenate([take(mat[2], self.right_index), take(mat[3], self.right_index)], 0)
+        first = iota((RANK, 128), 1) % (2 * RANK) < RANK
+        return jnp.concatenate([jnp.where(first, real, -imag), jnp.where(first, imag, real)], 0)
+
+    def inverse_root(self, mat):
+        eye = self.eye
+        square = sum(entry * entry for entry in mat)
+        norm = jnp.sqrt(2.0 * jnp.sum(square, axis=1, keepdims=True))
+        inv_norm = 1.0 / norm
+        squared = self.product(self.left(mat), self.right(mat))
+        first = [entry * inv_norm for entry in mat]
+        inverse_state = [1.5 * one - 0.5 * entry for one, entry in zip(eye, first)]
+        root_state = [
+            1.5 * entry - 0.5 * (twice * (inv_norm * inv_norm)) for entry, twice in zip(first, squared)
+        ]
+        for step in range(1, NS_STEPS):
+            both = self.product(self.left(inverse_state), self.right(root_state))
+            factor = [1.5 * one - 0.5 * entry for one, entry in zip(eye, both)]
+            inverse_state = self.product(self.left(factor), self.right(inverse_state))
+            if step < NS_STEPS - 1:
+                root_state = self.product(self.left(root_state), self.right(factor))
+        scale = 1.0 / jnp.sqrt(norm)
+        return [entry * scale for entry in inverse_state]
 
 
 def kernel(
@@ -140,7 +203,7 @@
         ]
         for c in range(COMP)
     ]
-    for per_comp in loads:
+    for per_comp in loads[:2]:
         for copy in per_comp:
             copy.start()
 
@@ -185,16 +248,16 @@
     for c in range(COMP):
         for copy in loads[c]:
             copy.wait()
+        if c + 2 < COMP:
+            for copy in loads[c + 2]:
+                copy.start()
         weighted = (wide(filt[...], snap[c]) * root_weight).astype(jnp.bfloat16)
         outgoing[c] = weighted.reshape(groups, ROWS, width)
         if c == 0:
             pl.semaphore_wait(barrier, groups + shares - 2)
 
-        def send_block(i, carry):
+        for i in far_first(groups):
             block_copy(c, lax.rem(group + i, groups)).start()
-            return carry
-
-        lax.fori_loop(1, groups, send_block, 0)
         spectra[c, group] = outgoing[c, group]
 
     block = iota((block_total, lanes), 0)
@@ -236,12 +299,13 @@
             device_id_type=MESH,
         )
 
-    def send_part(i, carry):
-        peer = lax.rem(share + i, shares)
+    side = math.isqrt(shares)
+    peers = [
+        lax.rem(share // side + i, side) * side + lax.rem(share + j, side)
+        for i, j in grid_far_first(side)
+    ]
+    for peer in peers:
         gram_copy(gram_part.at[peer], gram_in.at[share], peer, gram_send, gram_recv).start()
-        return carry
-
-    lax.fori_loop(1, shares, send_part, 0)
     gram_in[share] = gram_part[share]
     others = pl.ds(0, shares - 1)
     next_share = lax.rem(share + 1, shares)
@@ -255,24 +319,22 @@
     partner = jnp.where(lane == iota((ROWS, lanes), 0) // SHARE, partner, -partner)
     gram[share] = (mine + partner) * (1.0 / (COMP * width * shares))
 
-    def send_row(i, carry):
-        gram_copy(gram.at[share], gram.at[share], lax.rem(share + i, shares), row_send, row_recv).start()
-        return carry
-
-    lax.fori_loop(1, shares, send_row, 0)
+    for peer in peers:
+        gram_copy(gram.at[share], gram.at[share], peer, row_send, row_recv).start()
     gram_copy(gram.at[others], gram.at[others], next_share, row_send, row_recv).wait_recv()
     matrix = gram[...].reshape(lanes, lanes)
 
     nxt = mm(coef, matrix)
     image = mm(nxt, matrix)
+    flat = Flat()
     for step in range(ITERS):
-        joined = mm_nt(nxt, jnp.concatenate([image] * 4, 0))
+        rows = mm_nt(nxt, jnp.concatenate([image[:RANK]] * 8, 0))
         if step < ITERS - 1:
             further = mm(image, matrix)
-            left = left_form(inverse_root(joined))
+        left = left_form(flat.embedded(flat.inverse_root(flat.from_rows(rows))))
+        if step < ITERS - 1:
             nxt, image = wide(left, right_form(image)), wide(left, right_form(further))
         else:
-            left = left_form(inverse_root(joined))
             coef, final = wide(left, right_form(nxt)), wide(left, right_form(image))
 
     squares = mm_nt(jnp.ones((ROWS, lanes), jnp.float32), jnp.concatenate([final * final] * 4, 0))
@@ -288,11 +350,8 @@
             device_id_type=MESH,
         )
 
-    def send_energy(i, carry):
+    for i in far_first(groups):
         energy_copy(energy.at[group], energy.at[group], lax.rem(group + i, groups)).start()
-        return carry
-
-    lax.fori_loop(1, groups, send_energy, 0)
 
     coef_low = coef.astype(jnp.bfloat16)
     inv_weight = 1.0 / root_weight
@@ -364,10 +423,15 @@
             collective_id=0, has_side_effects=True, vmem_limit_bytes=40 << 20
         ),
     )(
-        jnp.transpose(snapshots, (0, 2, 1, 3)),
-        jnp.asarray(dft_table()),
-        quadrature.reshape(1, width),
-        jnp.transpose(omega, (0, 1, 3, 2)),
+        *(
+            pltpu.with_memory_space_constraint(operand, pltpu.HBM)
+            for operand in (
+                jnp.transpose(snapshots, (0, 2, 1, 3)),
+                jnp.asarray(dft_table()),
+                quadrature.reshape(1, width),
+                jnp.transpose(omega, (0, 1, 3, 2)),
+            )
+        )
     )
     return jnp.transpose(modes, (0, 2, 1, 3))[None], energies
 

time: 53.2 us -> 44.6 us (0.84)
  local copies, waits for them, and re-layouts: 6.44 us -> 1.28 us
  Pallas kernels: 45.9 us -> 42.5 us
    unnamed x10 -> x2, local copies, waits for them, and re-layouts: 6.44 us -> 1.28 us
    pallas_call x1, Pallas kernels: 45.9 us -> 42.5 us  [per_device(): pl.pallas_call(functools.partial(kernel, groups, shares), out_shape=(jax....]
where the time goes in v1:
time: 44.6 us; the launch traced here: 44.4 us
  Pallas kernels  42.5 us (95%)
  local copies, waits for them, and re-layouts  1.28 us (3%)
  between operations  0.64 us (1%)
    pallas_call x1, Pallas kernels, per_device(): pl.pallas_call(functools.partial(kernel, groups, shares), out_shape=(jax....  42.5 us
    unnamed x2, local copies, waits for them, and re-layouts  1.28 us

profile of v1, /device:TPU:1, one launch (start us, length us, event | category | flops | bytes accessed | tf_op | source)
XLA Modules:
  0.0 44.4 jit_solution(13520349031165485135)
XLA Ops:
  0.6 42.5 %shard_map.59 = (f32[2,3,16,512]{3,2,1,0:T(8,128)S(1)}, f32[16,16]{1,0:T(8,128)S(1)}) custom-call(bf16[4,3,512,512]{3,2,1,0:T(8,128)(2,1)} %bitcast.7, bf16[32,512]{1,0:T(8,128)(2,1)} %constant.2.clone.table_hbm, f32[1,512]{1,0:T(1,128)} %bitcast.9, f32[16,2,16,64]{3,2,1,0:T(8,128)} %bitcast.8), custom_call_target="tpu_custom_call" | custom-call | tf_op jit(solution)/shard_map/pallas_call | solution.py:389
  43.1 0.7 %copy.8 = f32[1,2,16,3,512]{4,2,3,1,0:T(8,128)} copy(f32[1,2,16,3,512]{4,2,3,1,0:T(8,128)S(1)} %bitcast.6) | data formatting | bytes 393216
  43.8 0.6 %copy.9 = f32[16,16]{1,0:T(8,128)} copy(f32[16,16]{1,0:T(8,128)S(1)} %get-tuple-element.9) | data formatting | bytes 2048

commit v2 on v1

--- a/solution.py
+++ b/solution.py
@@ -17,6 +17,7 @@
 NS_STEPS = 14
 SHARE = 4
 ROWS = 2 * SHARE
+PARTS = ((0, 1), (1, 2))
 HIGHEST = lax.Precision.HIGHEST
 MESH = pl.DeviceIdType.MESH
 
@@ -166,9 +167,7 @@
     filt,
     outgoing,
     spectra,
-    gram_part,
     gram_in,
-    gram,
     energy,
     modes,
     small_sem,
@@ -177,8 +176,6 @@
     recv_sem,
     gram_send,
     gram_recv,
-    row_send,
-    row_recv,
     energy_send,
     energy_recv,
     store_sem,
@@ -188,6 +185,18 @@
     block_total = groups * SHARE
     lanes = groups * ROWS
     width = snap.shape[2]
+
+    barrier = pltpu.get_barrier_semaphore()
+    side = math.isqrt(shares)
+    group_peers = [lax.rem(group + i, groups) for i in far_first(groups)]
+    share_peers = [
+        lax.rem(share // side + i, side) * side + lax.rem(share + j, side)
+        for i, j in grid_far_first(side)
+    ]
+    for peer in group_peers:
+        pl.semaphore_signal(barrier, inc=1, device_id=(share, peer), device_id_type=MESH)
+    for peer in share_peers:
+        pl.semaphore_signal(barrier, inc=1, device_id=(peer, group), device_id_type=MESH)
 
     small = [
         pltpu.make_async_copy(table_hbm, table, small_sem.at[0]),
@@ -203,26 +212,10 @@
         ]
         for c in range(COMP)
     ]
-    for per_comp in loads[:2]:
+    for per_comp in loads:
         for copy in per_comp:
             copy.start()
 
-    barrier = pltpu.get_barrier_semaphore()
-
-    def greet_group(i, carry):
-        pl.semaphore_signal(
-            barrier, inc=1, device_id=(share, lax.rem(group + i, groups)), device_id_type=MESH
-        )
-        return carry
-
-    def greet_share(i, carry):
-        pl.semaphore_signal(
-            barrier, inc=1, device_id=(lax.rem(share + i, shares), group), device_id_type=MESH
-        )
-        return carry
-
-    lax.fori_loop(1, groups, greet_group, 0)
-    lax.fori_loop(1, shares, greet_share, 0)
 
     for copy in small:
         copy.wait()
@@ -235,30 +228,30 @@
         filt[:, b * NT : (b + 1) * NT] = wide(chosen, table[...]).astype(jnp.bfloat16)
     root_weight = jnp.sqrt(quad[...])
 
-    def block_copy(c, target):
+    def block_copy(part, source, landing, peer):
         return pltpu.make_async_remote_copy(
-            src_ref=outgoing.at[c, target],
-            dst_ref=spectra.at[c, group],
-            send_sem=send_sem.at[c],
-            recv_sem=recv_sem.at[c],
-            device_id=(share, target),
+            src_ref=source,
+            dst_ref=landing,
+            send_sem=send_sem.at[part],
+            recv_sem=recv_sem.at[part],
+            device_id=(share, peer),
             device_id_type=MESH,
         )
 
     for c in range(COMP):
         for copy in loads[c]:
             copy.wait()
-        if c + 2 < COMP:
-            for copy in loads[c + 2]:
-                copy.start()
         weighted = (wide(filt[...], snap[c]) * root_weight).astype(jnp.bfloat16)
-        outgoing[c] = weighted.reshape(groups, ROWS, width)
-        if c == 0:
-            pl.semaphore_wait(barrier, groups + shares - 2)
-
-        for i in far_first(groups):
-            block_copy(c, lax.rem(group + i, groups)).start()
-        spectra[c, group] = outgoing[c, group]
+        outgoing[:, c] = weighted.reshape(groups, ROWS, width)
+        for part, (begin, count) in enumerate(PARTS):
+            if c != begin + count - 1:
+                continue
+            if part == 0:
+                pl.semaphore_wait(barrier, groups + shares - 2)
+            comps = pl.ds(begin, count)
+            for peer in group_peers:
+                block_copy(part, outgoing.at[peer, comps], spectra.at[group, comps], peer).start()
+    spectra[group] = outgoing[group]
 
     block = iota((block_total, lanes), 0)
     lane = iota((block_total, lanes), 1)
@@ -271,58 +264,74 @@
         jnp.concatenate([-start_im, start_re], 0), imag_lanes
     )
 
-    def whole(c):
-        return spectra.at[c, pl.ds(0, groups - 1)]
-
+    other_groups = pl.ds(0, groups - 1)
+    arrivals = []
     total = jnp.zeros((lanes, lanes), jnp.float32)
-    for c in range(COMP):
-        pltpu.make_async_remote_copy(
-            src_ref=whole(c),
-            dst_ref=whole(c),
-            send_sem=send_sem.at[c],
-            recv_sem=recv_sem.at[c],
-            device_id=(share, lax.rem(group + 1, groups)),
-            device_id_type=MESH,
-        ).wait_recv()
-        rows = spectra[c].reshape(lanes, width)
-        total = total + mm_nt(rows, rows, None)
-
-    gram_part[...] = total.reshape(shares, ROWS, lanes)
-
-    def gram_copy(source, landing, peer, send, recv):
+    for part, (begin, count) in enumerate(PARTS):
+        landing = spectra.at[other_groups, pl.ds(begin, count)]
+        arrivals.append(block_copy(part, landing, landing, group_peers[0]))
+        arrivals[part].wait_recv()
+        for c in range(begin, begin + count):
+            rows = spectra[:, c].reshape(lanes, width)
+            total = total + mm_nt(rows, rows, None)
+
+    tile = (ROWS, lanes)
+    row_part = iota(tile, 0) // SHARE % 2
+    lane_part = iota(tile, 1) // SHARE % 2
+
+    def next_lanes(value):
+        return pltpu.roll(value, lanes - SHARE, 1)
+
+    def previous_lanes(value):
+        return pltpu.roll(value, SHARE, 1)
+
+    for t in range(groups // 4):
+        packed = jnp.zeros(tile, jnp.float32)
+        for slot in range(4):
+            row_slot, lane_slot = slot // 2, slot % 2
+            begin = (4 * t + slot) * ROWS
+            value = total[begin : begin + ROWS]
+            swapped = pltpu.roll(value, SHARE, 0)
+            less = swapped - value if row_slot else value - swapped
+            both = value + swapped
+            entry = previous_lanes(less) + both if lane_slot else less + next_lanes(both)
+            packed = jnp.where((row_part == row_slot) & (lane_part == lane_slot), entry, packed)
+        gram_in[share, t] = packed
+
+    def gram_copy(source, landing, peer):
         return pltpu.make_async_remote_copy(
             src_ref=source,
             dst_ref=landing,
-            send_sem=send,
-            recv_sem=recv,
+            send_sem=gram_send,
+            recv_sem=gram_recv,
             device_id=(peer, group),
             device_id_type=MESH,
         )
 
-    side = math.isqrt(shares)
-    peers = [
-        lax.rem(share // side + i, side) * side + lax.rem(share + j, side)
-        for i, j in grid_far_first(side)
-    ]
-    for peer in peers:
-        gram_copy(gram_part.at[peer], gram_in.at[share], peer, gram_send, gram_recv).start()
-    gram_in[share] = gram_part[share]
-    others = pl.ds(0, shares - 1)
-    next_share = lax.rem(share + 1, shares)
-    gram_copy(gram_in.at[others], gram_in.at[others], next_share, gram_send, gram_recv).wait_recv()
-    mine = jnp.sum(gram_in[...], axis=0)
-    rolled = pltpu.roll(mine, SHARE, 0)
-    lane = iota((ROWS, lanes), 1) // SHARE % 2
-    partner = jnp.where(
-        lane == 0, pltpu.roll(rolled, lanes - SHARE, 1), pltpu.roll(rolled, SHARE, 1)
-    )
-    partner = jnp.where(lane == iota((ROWS, lanes), 0) // SHARE, partner, -partner)
-    gram[share] = (mine + partner) * (1.0 / (COMP * width * shares))
-
-    for peer in peers:
-        gram_copy(gram.at[share], gram.at[share], peer, row_send, row_recv).start()
-    gram_copy(gram.at[others], gram.at[others], next_share, row_send, row_recv).wait_recv()
-    matrix = gram[...].reshape(lanes, lanes)
+    for peer in share_peers:
+        gram_copy(gram_in.at[share], gram_in.at[share], peer).start()
+    other_shares = pl.ds(0, shares - 1)
+    gram_arrivals = gram_copy(gram_in.at[other_shares], gram_in.at[other_shares], share_peers[0])
+    gram_arrivals.wait_recv()
+    packed = jnp.sum(gram_in[...], axis=0) * (1.0 / (COMP * width * shares))
+    unpacked = []
+    for t in range(groups // 4):
+        value = packed[t]
+        spread = [
+            jnp.where(lane_part == 0, value, previous_lanes(value)),
+            jnp.where(lane_part == 1, value, next_lanes(value)),
+        ]
+        for slot in range(4):
+            row_slot, lane_slot = slot // 2, slot % 2
+            value = spread[lane_slot]
+            unpacked.append(jnp.where(row_part == row_slot, value, pltpu.roll(value, SHARE, 0)))
+    unpacked = jnp.concatenate(unpacked, 0)
+    flipped = unpacked.T
+    row_part = iota((lanes, lanes), 0) // SHARE % 2
+    lane_part = iota((lanes, lanes), 1) // SHARE % 2
+    matrix = 0.5 * (
+        jnp.where(row_part > lane_part, -unpacked, unpacked) + jnp.where(row_part < lane_part, -flipped, flipped)
+    )
 
     nxt = mm(coef, matrix)
     image = mm(nxt, matrix)
@@ -350,34 +359,35 @@
             device_id_type=MESH,
         )
 
-    for i in far_first(groups):
-        energy_copy(energy.at[group], energy.at[group], lax.rem(group + i, groups)).start()
+    for peer in group_peers:
+        energy_copy(energy.at[group], energy.at[group], peer).start()
 
     coef_low = coef.astype(jnp.bfloat16)
     inv_weight = 1.0 / root_weight
     for c in range(COMP):
-        out = wide(coef_low, spectra[c].reshape(lanes, width)) * inv_weight
+        out = wide(coef_low, spectra[:, c].reshape(lanes, width)) * inv_weight
         modes[0, c] = out[:RANK]
         modes[1, c] = out[RANK:]
     store = pltpu.make_async_copy(modes, modes_hbm, store_sem)
     store.start()
 
-    other_groups = pl.ds(0, groups - 1)
-    next_group = lax.rem(group + 1, groups)
-    energy_copy(energy.at[other_groups], energy.at[other_groups], next_group).wait()
+    energy_copy(energy.at[other_groups], energy.at[other_groups], group_peers[0]).wait()
     energy_out[...] = energy[...].reshape(groups, 128)[:, :RANK]
-    gram_copy(gram_in.at[others], gram_in.at[others], next_share, gram_send, gram_recv).wait_send()
-    gram_copy(gram.at[others], gram.at[others], next_share, row_send, row_recv).wait_send()
-    for c in range(COMP):
-        pltpu.make_async_remote_copy(
-            src_ref=whole(c),
-            dst_ref=whole(c),
-            send_sem=send_sem.at[c],
-            recv_sem=recv_sem.at[c],
-            device_id=(share, next_group),
-            device_id_type=MESH,
-        ).wait_send()
+    gram_arrivals.wait_send()
+    for arrival in arrivals:
+        arrival.wait_send()
     store.wait()
+
+
+def finish(modes_in, energy_in, modes_out, energy_out, modes_sem, energy_sem):
+    copies = [
+        pltpu.make_async_copy(modes_in, modes_out, modes_sem),
+        pltpu.make_async_copy(energy_in, energy_out, energy_sem),
+    ]
+    for copy in copies:
+        copy.start()
+    for copy in copies:
+        copy.wait()
 
 
 def per_device(snapshots, quadrature, omega):
@@ -400,19 +410,15 @@
             pltpu.VMEM((1, width), jnp.float32),
             pltpu.VMEM((2, RANK, groups * SHARE), jnp.float32),
             pltpu.VMEM((lanes, SHARE * NT), jnp.bfloat16),
-            pltpu.VMEM((COMP, groups, ROWS, width), jnp.bfloat16),
-            pltpu.VMEM((COMP, groups, ROWS, width), jnp.bfloat16),
-            pltpu.VMEM((shares, ROWS, lanes), jnp.float32),
-            pltpu.VMEM((shares, ROWS, lanes), jnp.float32),
-            pltpu.VMEM((shares, ROWS, lanes), jnp.float32),
+            pltpu.VMEM((groups, COMP, ROWS, width), jnp.bfloat16),
+            pltpu.VMEM((groups, COMP, ROWS, width), jnp.bfloat16),
+            pltpu.VMEM((shares, groups // 4, ROWS, lanes), jnp.float32),
             pltpu.VMEM((groups, 1, 128), jnp.float32),
             pltpu.VMEM((2, COMP, RANK, width), jnp.float32),
             dma((3,)),
             dma((COMP, SHARE)),
-            dma((COMP,)),
-            dma((COMP,)),
-            dma(()),
-            dma(()),
+            dma((len(PARTS),)),
+            dma((len(PARTS),)),
             dma(()),
             dma(()),
             dma(()),
@@ -433,6 +439,19 @@
             )
         )
     )
+    modes, energies = pl.pallas_call(
+        finish,
+        out_shape=(
+            jax.ShapeDtypeStruct(modes.shape, modes.dtype),
+            jax.ShapeDtypeStruct(energies.shape, energies.dtype),
+        ),
+        in_specs=[pl.BlockSpec(memory_space=pltpu.VMEM)] * 2,
+        out_specs=(any_space, any_space),
+        scratch_shapes=[dma(()), dma(())],
+    )(
+        pltpu.with_memory_space_constraint(modes, pltpu.VMEM),
+        pltpu.with_memory_space_constraint(energies, pltpu.VMEM),
+    )
     return jnp.transpose(modes, (0, 2, 1, 3))[None], energies
 
 

time: 44.6 us -> 40.9 us (0.917)
  Pallas kernels: 42.5 us -> 40.2 us
  local copies, waits for them, and re-layouts: 1.28 us -> 0 us
    pallas_call x1, Pallas kernels: 42.5 us -> 39.5 us  [per_device(): pl.pallas_call(functools.partial(kernel, groups, shares), out_shape=(jax....]
    unnamed x2 -> x0, local copies, waits for them, and re-layouts: 1.28 us -> none
    pallas_call x0 -> x1, Pallas kernels: none -> 0.7 us  [per_device(): pl.pallas_call(finish, out_shape=(jax.ShapeDtypeStruct(modes.shape, modes...]
where the time goes in v2:
time: 40.9 us; the launch traced here: 40.8 us
  Pallas kernels  40.2 us (98%)
  between operations  0.64 us (2%)
    pallas_call x1, Pallas kernels, per_device(): pl.pallas_call(functools.partial(kernel, groups, shares), out_shape=(jax....  39.5 us

profile of v2, /device:TPU:1, one launch (start us, length us, event | category | flops | bytes accessed | tf_op | source)
XLA Modules:
  0.0 40.8 jit_solution(6803403412302223058)
XLA Ops:
  0.6 39.5 %shard_map.59 = (f32[2,3,16,512]{3,2,1,0:T(8,128)S(1)}, f32[16,16]{1,0:T(8,128)S(1)}) custom-call(bf16[4,3,512,512]{3,2,1,0:T(8,128)(2,1)} %bitcast.6, bf16[32,512]{1,0:T(8,128)(2,1)} %constant.2.clone.table_hbm, f32[1,512]{1,0:T(1,128)} %bitcast.8, f32[16,2,16,64]{3,2,1,0:T(8,128)} %bitcast.7), custom_call_target="tpu_custom_call" | custom-call | tf_op jit(solution)/shard_map/pallas_call | solution.py:399
  40.1 0.7 %shard_map.60 = (f32[2,3,16,512]{3,2,1,0:T(8,128)}, f32[16,16]{1,0:T(8,128)}) custom-call(f32[2,3,16,512]{3,2,1,0:T(8,128)S(1)} %get-tuple-element.6.modes_in, f32[16,16]{1,0:T(8,128)S(1)} %get-tuple-element.7.energy_in), custom_call_target="tpu_custom_call" | custom-call | tf_op jit(solution)/shard_map/pallas_call | solution.py:442

commit v3 on v2

--- a/solution.py
+++ b/solution.py
@@ -102,19 +102,19 @@
         ] + [zero, zero]
 
     def left(self, mat):
-        return [[[take(mat[2 * p + h], self.left_index[k]) for k in range(2)] for h in range(2)] for p in range(2)]
+        return [[take(entry, index) for entry in mat] for index in self.left_index]
 
     def right(self, mat):
-        return [[take(mat[2 * p + k], self.right_index) for k in range(2)] for p in range(2)]
+        return [take(entry, self.right_index) for entry in mat]
 
     def product(self, left, right):
         out = []
         for p in range(2):
             for h in range(2):
                 if p == 0:
-                    terms = [left[0][h][k] * right[0][k] - left[1][h][k] * right[1][k] for k in range(2)]
+                    terms = [left[k][h] * right[k] - left[k][2 + h] * right[2 + k] for k in range(2)]
                 else:
-                    terms = [left[0][h][k] * right[1][k] + left[1][h][k] * right[0][k] for k in range(2)]
+                    terms = [left[k][h] * right[2 + k] + left[k][2 + h] * right[k] for k in range(2)]
                 out.append(lane_sum_free(terms[0] + terms[1]))
         return out
 
@@ -132,21 +132,29 @@
 
     def inverse_root(self, mat):
         eye = self.eye
+        left_eye, right_eye = self.left(eye), self.right(eye)
+
+        def factor_of(one, entry):
+            return 1.5 * one - 0.5 * entry
+
         square = sum(entry * entry for entry in mat)
         norm = jnp.sqrt(2.0 * jnp.sum(square, axis=1, keepdims=True))
         inv_norm = 1.0 / norm
-        squared = self.product(self.left(mat), self.right(mat))
+        left = self.left(mat)
+        squared = self.product(left, self.right(mat))
         first = [entry * inv_norm for entry in mat]
-        inverse_state = [1.5 * one - 0.5 * entry for one, entry in zip(eye, first)]
-        root_state = [
-            1.5 * entry - 0.5 * (twice * (inv_norm * inv_norm)) for entry, twice in zip(first, squared)
-        ]
+        inverse_state = [factor_of(one, entry) for one, entry in zip(eye, first)]
+        partly = [1.5 * entry - 0.5 * (twice * (inv_norm * inv_norm)) for entry, twice in zip(first, squared)]
+        left_factor = [[factor_of(one, entry * inv_norm) for one, entry in zip(*pair)] for pair in zip(left_eye, left)]
+        both = self.product(left_factor, self.right(partly))
         for step in range(1, NS_STEPS):
-            both = self.product(self.left(inverse_state), self.right(root_state))
-            factor = [1.5 * one - 0.5 * entry for one, entry in zip(eye, both)]
-            inverse_state = self.product(self.left(factor), self.right(inverse_state))
+            left = self.left(both)
+            left_factor = [[factor_of(one, entry) for one, entry in zip(*pair)] for pair in zip(left_eye, left)]
             if step < NS_STEPS - 1:
-                root_state = self.product(self.left(root_state), self.right(factor))
+                right_factor = [factor_of(one, entry) for one, entry in zip(right_eye, self.right(both))]
+                partly = self.product(left, right_factor)
+                both = self.product(left_factor, self.right(partly))
+            inverse_state = self.product(left_factor, self.right(inverse_state))
         scale = 1.0 / jnp.sqrt(norm)
         return [entry * scale for entry in inverse_state]
 
@@ -336,12 +344,20 @@
     nxt = mm(coef, matrix)
     image = mm(nxt, matrix)
     flat = Flat()
+
+    def inner(first, second):
+        return flat.from_rows(mm_nt(first, jnp.concatenate([second[:RANK]] * 8, 0)))
+
+    small = inner(nxt, image)
     for step in range(ITERS):
-        rows = mm_nt(nxt, jnp.concatenate([image[:RANK]] * 8, 0))
         if step < ITERS - 1:
             further = mm(image, matrix)
-        left = left_form(flat.embedded(flat.inverse_root(flat.from_rows(rows))))
+            ahead = inner(image, further)
+        root = flat.inverse_root(small)
+        left = left_form(flat.embedded(root))
         if step < ITERS - 1:
+            small = flat.product(flat.left(root), flat.right(ahead))
+            small = flat.product(flat.left(small), flat.right(root))
             nxt, image = wide(left, right_form(image)), wide(left, right_form(further))
         else:
             coef, final = wide(left, right_form(nxt)), wide(left, right_form(image))

time: 40.9 us -> 40.3 us (0.985)
  Pallas kernels: 40.2 us -> 39.5 us
    pallas_call x1, Pallas kernels: 39.5 us -> 38.8 us  [per_device(): pl.pallas_call(functools.partial(kernel, groups, shares), out_shape=(jax....]
where the time goes in v3:
time: 40.3 us; the launch traced here: 40.2 us
  Pallas kernels  39.5 us (98%)
  between operations  0.64 us (2%)
    pallas_call x1, Pallas kernels, per_device(): pl.pallas_call(functools.partial(kernel, groups, shares), out_shape=(jax....  38.8 us

profile of v3, /device:TPU:1, one launch (start us, length us, event | category | flops | bytes accessed | tf_op | source)
XLA Modules:
  0.0 40.2 jit_solution(14359101795140802844)
XLA Ops:
  0.6 38.8 %shard_map.59 = (f32[2,3,16,512]{3,2,1,0:T(8,128)S(1)}, f32[16,16]{1,0:T(8,128)S(1)}) custom-call(bf16[4,3,512,512]{3,2,1,0:T(8,128)(2,1)} %bitcast.6, bf16[32,512]{1,0:T(8,128)(2,1)} %constant.2.clone.table_hbm, f32[1,512]{1,0:T(1,128)} %bitcast.8, f32[16,2,16,64]{3,2,1,0:T(8,128)} %bitcast.7), custom_call_target="tpu_custom_call" | custom-call | tf_op jit(solution)/shard_map/pallas_call | solution.py:415
  39.5 0.7 %shard_map.60 = (f32[2,3,16,512]{3,2,1,0:T(8,128)}, f32[16,16]{1,0:T(8,128)}) custom-call(f32[2,3,16,512]{3,2,1,0:T(8,128)S(1)} %get-tuple-element.6.modes_in, f32[16,16]{1,0:T(8,128)S(1)} %get-tuple-element.7.energy_in), custom_call_target="tpu_custom_call" | custom-call | tf_op jit(solution)/shard_map/pallas_call | solution.py:458

commit v4 on v3

--- a/solution.py
+++ b/solution.py
@@ -17,6 +17,8 @@
 NS_STEPS = 14
 SHARE = 4
 ROWS = 2 * SHARE
+LEFT_ORDER = (0, 0, 0, 1, 1, 2)
+RIGHT_ORDER = (0, 1, 2, 0, 1, 0)
 PARTS = ((0, 1), (1, 2))
 HIGHEST = lax.Precision.HIGHEST
 MESH = pl.DeviceIdType.MESH
@@ -73,6 +75,16 @@
 def right_form(value):
     high, mid, low = (piece.astype(jnp.bfloat16) for piece in pieces(value))
     return jnp.concatenate([high, mid, low, high, mid, high, high, high], axis=0)
+
+
+def lane_form(value, order):
+    parts = [piece.astype(jnp.bfloat16) for piece in pieces(value)]
+    return jnp.concatenate([parts[i] for i in order], axis=1)
+
+
+def sublane_form(value, order):
+    parts = [piece.astype(jnp.bfloat16) for piece in pieces(value)]
+    return jnp.concatenate([parts[i] for i in order], axis=0)
 
 
 def wide(left, right):
@@ -341,18 +353,23 @@
         jnp.where(row_part > lane_part, -unpacked, unpacked) + jnp.where(row_part < lane_part, -flipped, flipped)
     )
 
-    nxt = mm(coef, matrix)
-    image = mm(nxt, matrix)
+    wide_matrix = sublane_form(matrix, RIGHT_ORDER)
+    nxt = wide(lane_form(coef, LEFT_ORDER), wide_matrix)
+    image = wide(lane_form(nxt, LEFT_ORDER), wide_matrix)
     flat = Flat()
 
     def inner(first, second):
-        return flat.from_rows(mm_nt(first, jnp.concatenate([second[:RANK]] * 8, 0)))
+        return flat.from_rows(
+            mm_nt(lane_form(first, LEFT_ORDER), jnp.concatenate([lane_form(second[:RANK], RIGHT_ORDER)] * 8, 0), None)
+        )
 
     small = inner(nxt, image)
     for step in range(ITERS):
         if step < ITERS - 1:
-            further = mm(image, matrix)
+            further = wide(lane_form(image, LEFT_ORDER), wide_matrix)
             ahead = inner(image, further)
+        else:
+            level = inner(image, image)
         root = flat.inverse_root(small)
         left = left_form(flat.embedded(root))
         if step < ITERS - 1:
@@ -360,9 +377,14 @@
             small = flat.product(flat.left(small), flat.right(root))
             nxt, image = wide(left, right_form(image)), wide(left, right_form(further))
         else:
-            coef, final = wide(left, right_form(nxt)), wide(left, right_form(image))
-
-    squares = mm_nt(jnp.ones((ROWS, lanes), jnp.float32), jnp.concatenate([final * final] * 4, 0))
+            coef = wide(left, right_form(nxt))
+
+    rotated = flat.product(flat.left(root), flat.right(level))
+    summand = [rotated[h] * root[h] + rotated[2 + h] * root[2 + h] for h in range(2)]
+    lane, column = iota((128, 128), 0), iota((128, 128), 1)
+    squares = sum(
+        mm(summand[h], jnp.where(lane // RANK + 8 * h == column, 1.0, 0.0).astype(jnp.float32)) for h in range(2)
+    )
     energy[group] = squares[:1, :]
 
     def energy_copy(source, landing, peer):

time: 40.3 us -> 39.9 us (0.990)
  no operation moved by 1% of the time
where the time goes in v4:
time: 39.9 us
  Pallas kernels  39.2 us (98%)
  between operations  0.64 us (2%)
    pallas_call x1, Pallas kernels, per_device(): pl.pallas_call(functools.partial(kernel, groups, shares), out_shape=(jax....  38.5 us

profile of v4, /device:TPU:1, one launch (start us, length us, event | category | flops | bytes accessed | tf_op | source)
XLA Modules:
  0.0 39.9 jit_solution(3735997248817773251)
XLA Ops:
  0.6 38.5 %shard_map.59 = (f32[2,3,16,512]{3,2,1,0:T(8,128)S(1)}, f32[16,16]{1,0:T(8,128)S(1)}) custom-call(bf16[4,3,512,512]{3,2,1,0:T(8,128)(2,1)} %bitcast.6, bf16[32,512]{1,0:T(8,128)(2,1)} %constant.2.clone.table_hbm, f32[1,512]{1,0:T(1,128)} %bitcast.8, f32[16,2,16,64]{3,2,1,0:T(8,128)} %bitcast.7), custom_call_target="tpu_custom_call" | custom-call | tf_op jit(solution)/shard_map/pallas_call | solution.py:437
  39.2 0.7 %shard_map.60 = (f32[2,3,16,512]{3,2,1,0:T(8,128)}, f32[16,16]{1,0:T(8,128)}) custom-call(f32[2,3,16,512]{3,2,1,0:T(8,128)S(1)} %get-tuple-element.6.modes_in, f32[16,16]{1,0:T(8,128)S(1)} %get-tuple-element.7.energy_in), custom_call_target="tpu_custom_call" | custom-call | tf_op jit(solution)/shard_map/pallas_call | solution.py:480
